TPU v7x, 32 devices: a whole 2x2x4 slice. The times are simulated.
32 devices in a mesh: blk: 4 (over z), head: 2 (over core), clip: 4 (over y, x).
Axes of the slice: x: 2, y: 2, z: 4, core: 2. Of those that a mesh axis runs over, the one named last changes fastest.
Arguments:
- tokens: bfloat16 [4608, 1536], P(('clip', 'blk', 'head')), parts along dimension 0, may hold values from -6 to 6
- modulation: float32 [12, 1536], P('clip'), parts along dimension 0, may hold values from -3 to 3
- w_qkv: bfloat16 [1536, 3, 1536], P(None, None, 'head'), may hold values from -0.25 to 0.25
- w_out: bfloat16 [1536, 1536], P('head'), may hold values from -0.15625 to 0.15625
- w_cross: bfloat16 [1536, 1536], P(None, 'head'), may hold values from -0.15625 to 0.15625
- q_gain: float32 [128], replicated, may hold values from 0.5 to 6
- k_gain: float32 [128], replicated, may hold values from 0.5 to 6
- cross_gain: float32 [128], replicated, may hold values from 0.5 to 6
- scene_keys: bfloat16 [1024, 1536], P(('clip', 'blk'), 'head'), parts along dimension 0, may hold values from -40 to 40
- scene_values: bfloat16 [1024, 1536], P(('clip', 'blk'), 'head'), parts along dimension 0, may hold values from -6 to 6
Outputs:
- hidden: bfloat16 [4608, 1536], P(('clip', 'blk', 'head')), parts along dimension 0
- cross_context: bfloat16 [4608, 1536], P(('clip', 'blk'), 'head'), parts along dimension 0
There are 4 independent parts, one for each index of `clip`. A program takes and returns all parts, laid end to end along the dimension named above; an argument that names none is the same for every part. Nothing has to cross between parts.
All inputs are finite; a program needn't handle non-finite values.
Results may differ from a plain program's by a relative error of at most 0.015.
The roundings to bfloat16 on the way count: a program that leaves them out, or rounds other values in their place, can miss the bound.
Values may be sent and summed in bfloat16 or wider, within the bound.
No kernel may reach another device: no remote copies, remote signals or barrier semaphores. Data moves between devices by JAX's collectives and lax.ppermute only.
A program may use at most 128 MiB of HBM per device.

v0:
```python
import jax
import jax.numpy as jnp
from jax import lax
from jax.sharding import PartitionSpec as P

HD = 128


def head_norm(values, gain):
    rms = jnp.mean(values * values, axis=-1, keepdims=True)
    return values * lax.rsqrt(rms + 1e-06) * gain


def attend_block(carry, queries, keys_blk, values_blk):
    best, total, accum = carry
    count = keys_blk.shape[0]
    heads_here = queries.shape[1]
    width = queries.shape[2]
    keys_three = keys_blk.reshape(count, heads_here, width)
    values_three = values_blk.reshape(count, heads_here, width).astype(jnp.float32)
    scores = jnp.einsum("rhd,nhd->hrn", queries, keys_three, preferred_element_type=jnp.float32) * (
        1.0 / width**0.5
    )
    newbest = jnp.maximum(best, jnp.max(scores, axis=-1))
    factor = jnp.exp(best - newbest)
    weights = jnp.exp(scores - newbest[..., None])
    total = total * factor + jnp.sum(weights, axis=-1)
    accum = accum * jnp.transpose(factor)[..., None] + jnp.einsum(
        "hrn,nhd->rhd", weights, values_three
    )
    return (newbest, total, accum)


def attend_keys(carry, queries, keys_rows, values_rows):
    count = keys_rows.shape[0]
    if count > 1024 and count % 1024 == 0:
        blocks = count // 1024
        keys_split = keys_rows.reshape(blocks, 1024, keys_rows.shape[1])
        values_split = values_rows.reshape(blocks, 1024, values_rows.shape[1])

        def advance(state, pair):
            return (attend_block(state, queries, pair[0], pair[1]), None)

        carry, unused = lax.scan(advance, carry, (keys_split, values_split))
        return carry
    return attend_block(carry, queries, keys_rows, values_rows)


def start_state(queries):
    rows = queries.shape[0]
    heads_here = queries.shape[1]
    best = jnp.full((heads_here, rows), -1e30, jnp.float32)
    total = jnp.zeros((heads_here, rows), jnp.float32)
    accum = jnp.zeros(queries.shape, jnp.float32)
    return (best, total, accum)


def finish_state(state):
    best, total, accum = state
    result = accum / jnp.transpose(total)[..., None]
    return result.reshape(result.shape[0], result.shape[1] * result.shape[2]).astype(jnp.bfloat16)


def shards(
    tokens, modulation, w_qkv, w_out, w_cross, q_gain, k_gain, cross_gain, scene_keys, scene_values
):
    width = tokens.shape[1]
    local_width = w_qkv.shape[2]
    heads_here = local_width // HD
    rows_raw = lax.all_gather(tokens, "head", axis=0, tiled=True)
    rows_count = rows_raw.shape[0]
    xfloat = rows_raw.astype(jnp.float32)
    mean = jnp.mean(xfloat, axis=-1, keepdims=True)
    var = jnp.mean((xfloat - mean) ** 2, axis=-1, keepdims=True)
    normed = (xfloat - mean) * lax.rsqrt(var + 1e-06)
    modulated = (normed * (1.0 + modulation[1]) + modulation[0]).astype(jnp.bfloat16)
    projected = jnp.dot(
        modulated, w_qkv.reshape(width, 3 * local_width), preferred_element_type=jnp.float32
    )
    projected = projected.reshape(rows_count, 3, heads_here, HD)
    queries = head_norm(projected[:, 0], q_gain).astype(jnp.bfloat16)
    keys_flat = (
        head_norm(projected[:, 1], k_gain).astype(jnp.bfloat16).reshape(rows_count, local_width)
    )
    values_flat = projected[:, 2].astype(jnp.bfloat16).reshape(rows_count, local_width)
    pieces = (
        lax.all_gather(keys_flat, "blk", axis=0, tiled=True),
        lax.all_gather(values_flat, "blk", axis=0, tiled=True),
    )
    state = attend_keys(start_state(queries), queries, pieces[0], pieces[1])
    context = finish_state(state)
    partial_sum = jnp.dot(context, w_out, preferred_element_type=jnp.float32)
    mine = lax.psum_scatter(partial_sum, "head", scatter_dimension=0, tiled=True)
    hidden = (tokens.astype(jnp.float32) + modulation[2] * mine).astype(jnp.bfloat16)
    hidden_all = lax.all_gather(hidden, "head", axis=0, tiled=True)
    cross_proj = jnp.dot(hidden_all, w_cross, preferred_element_type=jnp.float32).reshape(
        rows_count, heads_here, HD
    )
    cross_queries = head_norm(cross_proj, cross_gain).astype(jnp.bfloat16)
    pieces = (
        lax.all_gather(scene_keys, "blk", axis=0, tiled=True),
        lax.all_gather(scene_values, "blk", axis=0, tiled=True),
    )
    scene_state = attend_keys(start_state(cross_queries), cross_queries, pieces[0], pieces[1])
    cross_context = finish_state(scene_state)
    return (hidden, cross_context)


def solution(mesh):
    return jax.shard_map(
        shards,
        mesh=mesh,
        in_specs=(
            P(("clip", "blk", "head"), None),
            P("clip", None),
            P(None, None, "head"),
            P("head", None),
            P(None, "head"),
            P(),
            P(),
            P(),
            P(("clip", "blk"), "head"),
            P(("clip", "blk"), "head"),
        ),
        out_specs=(P(("clip", "blk", "head"), None), P(("clip", "blk"), "head")),
        check_vma=False,
    )
```

profile of v0, /device:TPU:0, one launch (start us, length us, event | category | flops | bytes accessed | tf_op | source)
XLA Modules:
  0.0 181.9 jit_solution(1748630479518706990)
XLA Ops:
  7.2 2.9 %all_gather.18 = bf16[288,1536]{1,0:T(8,128)(2,1)S(1)} all-gather(bf16[144,1536]{1,0:T(8,128)(2,1)} %param.10), channel_id=1, replica_groups=mesh['blk'=4,'head'=2,'clip'=4] {'head'}, dimensions={0}, use_global_device_ids=true | all-gather | bytes 1327104 | tf_op jit(solution)/shard_map/all_gather | solution.py:70
  10.8 10.3 %copy.45 = bf16[1536,3,768]{0,2,1:T(8,128)(2,1)} copy(bf16[1536,3,768]{2,0,1:T(8,128)(2,1)} %param.12) | data formatting | bytes 14155776 | tf_op args[2]
  21.1 5.0 %fusion.23 = f32[288,3,6,128]{3,0,2,1:T(8,128)S(1)} fusion(bf16[3,6,128,1536]{3,2,1,0:T(8,128)(2,1)} %bitcast.93, bf16[288,1536]{1,0:T(8,128)(2,1)S(1)} %all_gather.18, f32[1536]{0:T(1024)S(1)} %get-tuple-element.3, f32[1536]{0:T(1024)S(1)} %get-tuple-element.4, f32[288]{0:T(512)S(1)} %add_rsqrt_fusion.3, f32[288]{0:T(512)S(1)} %broadcast_multiply_fusion), kind=kOutput, calls=%fused_computation.31 | convolution fusion | flops 2041085952 | bytes 10631424 | tf_op jit(solution)/shard_map/dot_general | solution.py:77
  26.1 1.5 copy-done.2
  29.1 1.0 fusion.26
  30.2 1.2 slice.39
  31.7 0.8 copy.84
  32.6 1.6 multiply_reduce_fusion.4
  34.1 39.0 %all-gather.3.cloned.1.call-done = bf16[1152,768]{1,0:T(8,128)(2,1)} async-done(((bf16[288,768]{1,0:T(8,128)(2,1)}), bf16[1152,768]{1,0:T(8,128)(2,1)}) %all-gather.3.cloned.1.call-update) | async-done | bytes 1769488 | tf_op jit(solution)/shard_map/all_gather | solution.py:87
  73.2 3.9 %copy.48 = bf16[1152,768]{0,1:T(8,128)(2,1)} copy(bf16[1152,768]{1,0:T(8,128)(2,1)} %all-gather.3.cloned.1.call-done) | data formatting | bytes 3538944 | tf_op jit(solution)/shard_map/all_gather | solution.py:87
  77.0 3.1 %multiply_reduce_fusion = (f32[6,288]{1,0:T(8,128)S(1)}, f32[6,288,1152]{2,1,0:T(8,128)S(1)}) fusion(bf16[1152,6,128]{0,2,1:T(8,128)(2,1)} %bitcast.94, f32[288,3,6,128]{3,0,2,1:T(8,128)} %copy-done.2, f32[128]{0:T(128)S(1)} %copy-done.10, f32[288,6]{0,1:T(8,128)S(1)} %add_rsqrt_fusion.2), kind=kOutput, calls=%fused_computation.1 | convolution fusion | flops 514251072 | bytes 10631168 | tf_op jit(solution)/shard_map/rhd,nhd->hrn/dot_general | solution.py:21
  80.2 1.8 %fusion = f32[6,288]{1,0:T(8,128)S(1)} fusion(f32[6,288,1152]{2,1,0:T(8,128)S(1)} %get-tuple-element.12, f32[6,288]{1,0:T(8,128)S(1)} %get-tuple-element.10), kind=kLoop, calls=%fused_computation.2 | loop fusion | flops 5970240 | bytes 7976448 | tf_op jit(solution)/shard_map/reduce_sum | solution.py:27
  82.0 1.2 copy-done.1
  83.3 31.2 %all-gather.5.cloned.1.call-done = bf16[1152,768]{1,0:T(8,128)(2,1)} async-done(((bf16[288,768]{1,0:T(8,128)(2,1)}), bf16[1152,768]{1,0:T(8,128)(2,1)}) %all-gather.5.cloned.1.call-update) | async-done | bytes 1769488 | tf_op jit(solution)/shard_map/all_gather | solution.py:88
  114.4 3.9 %copy.51 = bf16[1152,768]{0,1:T(8,128)(2,1)} copy(bf16[1152,768]{1,0:T(8,128)(2,1)} %all-gather.5.cloned.1.call-done) | data formatting | bytes 3538944 | tf_op jit(solution)/shard_map/all_gather | solution.py:88
  118.3 5.4 %fusion.21 = bf16[6,36,8,128]{3,2,1,0:T(8,128)(2,1)S(1)} fusion(bf16[1152,6,128]{0,2,1:T(8,128)(2,1)} %bitcast.98, f32[6,288,1152]{2,1,0:T(8,128)} %copy-done.1, f32[6,288]{1,0:T(8,128)S(1)} %get-tuple-element.10, f32[288,6]{0,1:T(8,128)S(1)} %bitcast_add_fusion.1, f32[288,6]{0,1:T(8,128)S(1)} %get-tuple-element.9), kind=kOutput, calls=%fused_computation.29 | convolution fusion | flops 514252800 | bytes 10195200 | tf_op jit(solution)/shard_map/hrn,nhd->rhd/dot_general | solution.py:28
  123.7 2.1 %fusion.34 = f32[288,1536]{1,0:T(8,128)} fusion(bf16[768,1536]{1,0:T(8,128)(2,1)S(1)} %copy-done, bf16[6,36,8,128]{3,2,1,0:T(8,128)(2,1)S(1)} %fusion.21), kind=kOutput, calls=%fused_computation.50 | convolution fusion | flops 679477248 | bytes 4571136 | tf_op jit(solution)/shard_map/dot_general | solution.py:92
  125.8 0.9 copy-done.7
  126.7 15.4 %all_gather.22 = bf16[256,768]{1,0:T(8,128)(2,1)S(1)} all-gather(bf16[64,768]{1,0:T(8,128)(2,1)S(1)} %copy-done.7), channel_id=1, replica_groups=mesh['blk'=4,'head'=2,'clip'=4] {'blk'}, dimensions={0}, use_global_device_ids=true | all-gather | bytes 491520 | tf_op jit(solution)/shard_map/all_gather | solution.py:101
  142.1 0.9 copy.56
  143.0 14.9 %all_gather.23 = bf16[256,768]{1,0:T(8,128)(2,1)S(1)} all-gather(bf16[64,768]{1,0:T(8,128)(2,1)S(1)} %copy-done.8), channel_id=1, replica_groups=mesh['blk'=4,'head'=2,'clip'=4] {'blk'}, dimensions={0}, use_global_device_ids=true | all-gather | bytes 491520 | tf_op jit(solution)/shard_map/all_gather | solution.py:102
  157.9 0.9 copy.59
  158.9 1.4 add_convert_fusion
  161.1 2.6 %all_gather.21 = bf16[288,1536]{1,0:T(8,128)(2,1)S(1)} all-gather(bf16[144,1536]{1,0:T(8,128)(2,1)S(1)} %add_convert_fusion), channel_id=1, replica_groups=mesh['blk'=4,'head'=2,'clip'=4] {'head'}, dimensions={0}, use_global_device_ids=true | all-gather | bytes 1327104 | tf_op jit(solution)/shard_map/all_gather | solution.py:95
  163.7 1.8 fusion.44
  165.5 1.3 reshape.88
  166.8 1.0 multiply_reduce_fusion.2
  167.8 1.0 copy.54
  169.4 1.5 copy.55
  170.9 1.3 multiply_convert_fusion
  173.6 0.9 fusion.18
  174.5 0.8 copy.85
  (52 shorter events, 5.2 us)
Async XLA Ops:
  7.2 116.6 %copy-start = (bf16[768,1536]{1,0:T(8,128)(2,1)S(1)}, bf16[768,1536]{1,0:T(8,128)(2,1)}, u32[]{:S(2)}) copy-start(bf16[768,1536]{1,0:T(8,128)(2,1)} %param.13) | copy-start | bytes 7077892
  7.2 3.6 %copy-start.9 = (f32[3,1536]{1,0:T(4,128)S(1)}, f32[3,1536]{1,0:T(4,128)}, u32[]{:S(2)}) copy-start(f32[3,1536]{1,0:T(4,128)} %param.11) | copy-start | bytes 55300
  7.2 66.0 %all-gather.3.cloned.1.call-start = ((), (), s32[]{:S(2)}) async-start(), calls=%async_computation.1 | async-start | bytes 2211840 | tf_op jit(solution)/shard_map/all_gather | solution.py:87
  26.1 1.5 copy-start.2
  27.6 1.1 copy-start.12
  30.2 84.3 %all-gather.5.cloned.1.call-start = ((), (), s32[]{:S(2)}) async-start(), calls=%async_computation.2 | async-start | bytes 2211840 | tf_op jit(solution)/shard_map/all_gather | solution.py:88
  32.5 126.4 %reduce-scatter.2.cloned.1.call-start = ((), (), s32[]{:S(2)}) async-start(), calls=%async_computation.3 | async-start | bytes 2654208 | tf_op jit(solution)/shard_map/reduce_scatter | solution.py:93
  34.1 42.9 %copy-start.10 = (f32[128]{0:T(128)S(1)}, f32[128]{0:T(128)}, u32[]{:S(2)}) copy-start(f32[128]{0:T(128)} %param.15) | copy-start | bytes 1540
  80.2 3.1 %copy-start.1 = (f32[6,288,1152]{2,1,0:T(8,128)}, f32[6,288,1152]{2,1,0:T(8,128)S(1)}, u32[]{:S(2)}) copy-start(f32[6,288,1152]{2,1,0:T(8,128)S(1)} %get-tuple-element.12) | copy-start | bytes 23887876
  125.8 0.9 copy-start.7
  125.8 17.2 %copy-start.8 = (bf16[64,768]{1,0:T(8,128)(2,1)S(1)}, bf16[64,768]{1,0:T(8,128)(2,1)}, u32[]{:S(2)}) copy-start(bf16[64,768]{1,0:T(8,128)(2,1)} %param.19) | copy-start | bytes 294916
  125.8 33.1 %copy-start.3 = (bf16[144,1536]{1,0:T(8,128)(2,1)S(1)}, bf16[144,1536]{1,0:T(8,128)(2,1)}, u32[]{:S(2)}) copy-start(bf16[144,1536]{1,0:T(8,128)(2,1)} %param.10) | copy-start | bytes 1327108
  158.9 4.8 %copy-start.13 = (bf16[1536,768]{1,0:T(8,128)(2,1)S(1)}, bf16[1536,768]{1,0:T(8,128)(2,1)}, u32[]{:S(2)}) copy-start(bf16[1536,768]{1,0:T(8,128)(2,1)} %param.14) | copy-start | bytes 7077892
  160.3 0.8 copy-start.4
  165.4 5.5 %copy-start.11 = (f32[128]{0:T(128)S(1)}, f32[128]{0:T(128)}, u32[]{:S(2)}) copy-start(f32[128]{0:T(128)} %param.17) | copy-start | bytes 1540
  170.9 1.3 copy-start.5
  172.3 1.3 copy-start.6
Sparse Core Ops, SparseCore 0:
  30.3 42.8 all-gather.2
  75.3 39.0 all-gather.4
  126.0 8.1 reduce-scatter.1
where the time goes:
time: 183 us; the launch traced here: 182 us
  waiting for transfers between devices  70.3 us (38%)
  blocking collectives  35.8 us (20%)
  local copies, waits for them, and re-layouts  32.2 us (18%)
  matrix products  18.8 us (10%)
  between operations  14 us (8%)
  other arithmetic  10.7 us (6%)
    all_gather x1, waiting for transfers between devices, shards(): lax.all_gather(keys_flat, 'blk', axis=0, tiled=True)  39 us
    all_gather x1, waiting for transfers between devices, shards(): lax.all_gather(values_flat, 'blk', axis=0, tiled=True)  31.2 us
    unnamed x30, local copies, waits for them, and re-layouts  15.5 us
    all_gather x1, blocking collectives, shards(): lax.all_gather(scene_keys, 'blk', axis=0, tiled=True)  15.4 us
    all_gather x1, blocking collectives, shards(): lax.all_gather(scene_values, 'blk', axis=0, tiled=True)  14.9 us
    dot_general x2, matrix products, attend_block(): jnp.einsum('hrn,nhd->rhd', weights, values_three)  6.29 us
    dot_general x1, matrix products, shards(): jnp.dot(modulated, w_qkv.reshape(width, 3 * local_width), preferred_eleme...  4.98 us
    all_gather x1, local copies, waits for them, and re-layouts, shards(): lax.all_gather(values_flat, 'blk', axis=0, tiled=True)  3.88 us
  transfers between devices with their start and end apart: 3, of which 2 were waited for; matrix products, arithmetic and copies ran while one was open for 8% of the time, Pallas kernels for 0%

commit v1 on v0

v1 whole, which is shorter than its diff:
```python
import functools
import math

import jax
import jax.numpy as jnp
from jax import lax
from jax.experimental import pallas as pl
from jax.experimental.pallas import tpu as pltpu
from jax.sharding import PartitionSpec as P

HD = 128
EPS = 1e-06


def modulate(rows, mod_ref):
    xfloat = rows.astype(jnp.float32)
    mean = jnp.mean(xfloat, axis=-1, keepdims=True)
    centred = xfloat - mean
    var = jnp.mean(centred * centred, axis=-1, keepdims=True)
    normed = centred * lax.rsqrt(var + EPS)
    return (normed * (1.0 + mod_ref[1:2, :]) + mod_ref[0:1, :]).astype(jnp.bfloat16)


def head_norm(values, gain):
    rms = jnp.mean(values * values, axis=-1, keepdims=True)
    return (values * lax.rsqrt(rms + EPS) * gain).astype(jnp.bfloat16)


def dot(left, right):
    return jnp.dot(left, right, preferred_element_type=jnp.float32)


def dot_t(left, right):
    return lax.dot_general(
        left, right, (((1,), (1,)), ((), ())), preferred_element_type=jnp.float32
    )


def column_step(width):
    return 2 * HD if width % (2 * HD) == 0 else HD


def blocks_kernel(n_rows, first, last, scale, *refs):
    refs = list(refs)
    row_refs = [refs.pop(0) for _ in range(n_rows)]
    mod_ref, w_ref, kg_ref = refs.pop(0), refs.pop(0), refs.pop(0)
    if first:
        qg_ref = refs.pop(0)
    else:
        q_ref, state_in, acc_in = refs.pop(0), refs.pop(0), refs.pop(0)
    if last:
        ctx_ref = refs.pop(0)
    else:
        if first:
            q_ref = refs.pop(0)
        state_out, acc_out = refs.pop(0), refs.pop(0)
    rows_ref = refs.pop(0)
    at = 0
    for ref in row_refs:
        count = ref.shape[0]
        rows_ref[at : at + count, :] = modulate(ref[...], mod_ref)
        at += count
    width = w_ref.shape[2]
    wide = column_step(width)
    rows = rows_ref[...]
    for c in range(0, width, wide):
        if first:
            q_wide = dot(rows, w_ref[0, :, c : c + wide])
        k_wide = dot(rows, w_ref[1, :, c : c + wide])
        v_wide = dot(rows, w_ref[2, :, c : c + wide]).astype(jnp.bfloat16)
        for j in range(0, wide, HD):
            h = (c + j) // HD
            lanes = slice(c + j, c + j + HD)
            keys = head_norm(k_wide[:, j : j + HD], kg_ref[...])
            values = v_wide[:, j : j + HD]
            if first:
                queries = head_norm(q_wide[:, j : j + HD], qg_ref[...])
                q_ref[:, lanes] = queries
            else:
                queries = q_ref[:, lanes]
            scores = dot_t(queries, keys)
            best = jnp.max(scores, axis=-1, keepdims=True)
            if not first:
                before = state_in[:, 2 * h : 2 * h + 1]
                best = jnp.maximum(best, before)
            weights = jnp.exp((scores - best) * scale)
            total = jnp.sum(weights, axis=-1, keepdims=True)
            accum = dot(weights.astype(jnp.bfloat16), values)
            if not first:
                factor = jnp.exp((before - best) * scale)
                total = total + factor * state_in[:, 2 * h + 1 : 2 * h + 2]
                accum = accum + factor * acc_in[:, lanes]
            if last:
                ctx_ref[:, lanes] = (accum / total).astype(jnp.bfloat16)
            else:
                state_out[:, 2 * h : 2 * h + 1] = best
                state_out[:, 2 * h + 1 : 2 * h + 2] = total
                acc_out[:, lanes] = accum


def final_kernel(
    n_scene, scale,
    me_ref, ctx_ref, ctx_p_ref, own_ref, other_ref, mod_ref, wo_ref, wo_p_ref, wc_ref, cg_ref, *refs
):
    scene_refs = refs[:n_scene]
    hidden_ref, out_ref, hid_ref, keys_ref = refs[n_scene:]
    half = own_ref.shape[0]
    width = ctx_ref.shape[1]
    model = own_ref.shape[1]
    wide = column_step(width)
    swapped = jnp.concatenate([ctx_p_ref[half:, :], ctx_p_ref[:half, :]], axis=0)
    mine = ctx_ref[...]
    for c in range(0, model, wide):
        cols = slice(c, c + wide)
        attn = dot(mine, wo_ref[:, cols]) + dot(swapped, wo_p_ref[:, cols])
        gated = mod_ref[2:3, cols] * attn
        own = (own_ref[:, cols].astype(jnp.float32) + gated[:half]).astype(jnp.bfloat16)
        hidden_ref[:, cols] = own
        hid_ref[:half, cols] = own
        hid_ref[half:, cols] = (
            other_ref[:, cols].astype(jnp.float32) + gated[half:]
        ).astype(jnp.bfloat16)
    each = scene_refs[0].shape[0] // 2
    for i, ref in enumerate(scene_refs):
        keys_ref[0, i * each : (i + 1) * each, :] = ref[:each, :]
        keys_ref[1, i * each : (i + 1) * each, :] = ref[each:, :]
    rows = hid_ref[...]
    me = me_ref[0]
    at_own = pl.multiple_of(me * half, half)
    at_other = pl.multiple_of((1 - me) * half, half)
    for c in range(0, width, wide):
        q_wide = dot(rows, wc_ref[:, c : c + wide])
        for j in range(0, wide, HD):
            lanes = slice(c + j, c + j + HD)
            queries = head_norm(q_wide[:, j : j + HD], cg_ref[...])
            scores = dot_t(queries, keys_ref[0, :, lanes])
            best = jnp.max(scores, axis=-1, keepdims=True)
            weights = jnp.exp((scores - best) * scale)
            total = jnp.sum(weights, axis=-1, keepdims=True)
            accum = dot(weights.astype(jnp.bfloat16), keys_ref[1, :, lanes])
            result = (accum / total).astype(jnp.bfloat16)
            out_ref[pl.ds(at_own, half), lanes] = result[:half]
            out_ref[pl.ds(at_other, half), lanes] = result[half:]


VM = pl.BlockSpec(memory_space=pltpu.VMEM)
SM = pl.BlockSpec(memory_space=pltpu.SMEM)
PARAMS = pltpu.CompilerParams(vmem_limit_bytes=48 * 1024 * 1024)


def blocks_call(row_list, mod, w3, q_gain, k_gain, carry, last, name):
    first = carry is None
    model = row_list[0].shape[1]
    keys = sum(r.shape[0] for r in row_list)
    width = w3.shape[2]
    rows_q = keys if first else carry[0].shape[0]
    args = list(row_list) + [mod, w3, k_gain]
    args += [q_gain] if first else list(carry)
    shapes = []
    if last:
        shapes.append(jax.ShapeDtypeStruct((rows_q, width), jnp.bfloat16))
    else:
        if first:
            shapes.append(jax.ShapeDtypeStruct((rows_q, width), jnp.bfloat16))
        shapes.append(jax.ShapeDtypeStruct((rows_q, HD), jnp.float32))
        shapes.append(jax.ShapeDtypeStruct((rows_q, width), jnp.float32))
    flops = 2 * keys * model * width * (3 if first else 2) + 4 * rows_q * keys * width
    out = pl.pallas_call(
        functools.partial(
            blocks_kernel, len(row_list), first, last, 1.0 / math.sqrt(HD)
        ),
        out_shape=shapes,
        in_specs=[VM] * len(args),
        out_specs=[VM] * len(shapes),
        scratch_shapes=[pltpu.VMEM((keys, model), jnp.bfloat16)],
        compiler_params=PARAMS,
        cost_estimate=pl.CostEstimate(
            flops=flops,
            transcendentals=rows_q * keys * width // HD,
            bytes_accessed=2 * keys * model + 6 * model * width,
        ),
        name=name,
    )(*args)
    if last:
        return out[0]
    return tuple(out) if first else (carry[0],) + tuple(out)


def final_call(me, ctx, ctx_p, own, other, mod, wo, wo_p, wc, cg, scenes):
    half, model = own.shape
    rows, width = ctx.shape
    each = scenes[0].shape[0] // 2
    args = [me, ctx, ctx_p, own, other, mod, wo, wo_p, wc, cg] + list(scenes)
    flops = 4 * rows * model * width + 2 * rows * model * width
    return pl.pallas_call(
        functools.partial(final_kernel, len(scenes), 1.0 / math.sqrt(HD)),
        out_shape=[
            jax.ShapeDtypeStruct((half, model), jnp.bfloat16),
            jax.ShapeDtypeStruct((rows, width), jnp.bfloat16),
        ],
        in_specs=[SM] + [VM] * (len(args) - 1),
        out_specs=[VM, VM],
        scratch_shapes=[
            pltpu.VMEM((rows, model), jnp.bfloat16),
            pltpu.VMEM((2, each * len(scenes), width), jnp.bfloat16),
        ],
        compiler_params=PARAMS,
        cost_estimate=pl.CostEstimate(
            flops=flops,
            transcendentals=rows * each * len(scenes) * width // HD,
            bytes_accessed=6 * model * width,
        ),
        name="final",
    )(*args)


def swap_cores(x):
    return lax.ppermute(x, "head", [(0, 1), (1, 0)])


def shards(
    tokens, modulation, w_qkv, w_out, w_cross, q_gain, k_gain, cross_gain, scene_keys, scene_values
):
    count = lax.axis_size("blk")
    me = lax.axis_index("head").astype(jnp.int32).reshape(1)
    place = lax.axis_index("blk")
    w3 = jnp.transpose(w_qkv, (1, 0, 2))
    q_gain, k_gain, cross_gain = (g.reshape(1, HD) for g in (q_gain, k_gain, cross_gain))
    scene = jnp.concatenate([scene_keys, scene_values], axis=0)
    other = swap_cores(tokens)
    w_out_p = swap_cores(w_out)
    if count == 4:
        xor1 = [(i, i ^ 1) for i in range(4)]
        xor2 = [(i, i ^ 2) for i in range(4)]
        inner = [(1, 2), (2, 1)]
        outer = [(1, 0), (2, 3)]
        at_end = (place == 0) | (place == count - 1)

        def gather(x):
            near = lax.ppermute(x, "blk", xor1)
            far = lax.ppermute(x, "blk", xor2)
            mid = lax.ppermute(x, "blk", inner)
            out = lax.ppermute(far, "blk", outer)
            return [near, far, jnp.where(at_end, out, mid)]
    else:

        def gather(x):
            return [
                lax.ppermute(x, "blk", [(i, (i + s) % count) for i in range(count)])
                for s in range(1, count)
            ]

    slots = gather(tokens)
    scenes = [scene] + gather(scene)
    pairs = [(x, swap_cores(x)) for x in slots]
    carry = blocks_call(
        [tokens, other], modulation, w3, q_gain, k_gain, None, count == 1, "own"
    )
    while pairs:
        taken, pairs = (pairs[:2], pairs[2:]) if len(pairs) > 1 else (pairs, [])
        carry = blocks_call(
            [r for pair in taken for r in pair],
            modulation, w3, q_gain, k_gain, carry, not pairs, "more" if pairs else "last",
        )
    ctx = carry
    ctx_p = swap_cores(ctx)
    hidden, cross_context = final_call(
        me, ctx, ctx_p, tokens, other, modulation, w_out, w_out_p, w_cross, cross_gain, scenes
    )
    return (hidden, cross_context)


def solution(mesh):
    return jax.shard_map(
        shards,
        mesh=mesh,
        in_specs=(
            P(("clip", "blk", "head"), None),
            P("clip", None),
            P(None, None, "head"),
            P("head", None),
            P(None, "head"),
            P(),
            P(),
            P(),
            P(("clip", "blk"), "head"),
            P(("clip", "blk"), "head"),
        ),
        out_specs=(P(("clip", "blk", "head"), None), P(("clip", "blk"), "head")),
        check_vma=False,
    )
```

time: 183 us -> 97.1 us (0.53)
  the two profiles are of different devices: /device:TPU:0 before, /device:TPU:26 now
where the time goes in v1:
time: 97.1 us; the launch traced here: 96.6 us
  waiting for transfers between devices  41.3 us (43%)
  Pallas kernels  35.3 us (36%)
  starting transfers between devices  12.3 us (13%)
  local copies, waits for them, and re-layouts  5.9 us (6%)
  other arithmetic  1 us (1%)
    pallas_call x3, Pallas kernels, blocks_call(): pl.pallas_call(functools.partial(blocks_kernel, len(row_list), first, las...  27 us
    ppermute x2, waiting for transfers between devices, gather(): far = lax.ppermute(x, 'blk', xor2)  21 us
    ppermute x2, waiting for transfers between devices, gather(): out = lax.ppermute(far, 'blk', outer)  17.5 us
    pallas_call x1, Pallas kernels, final_call(): pl.pallas_call(functools.partial(final_kernel, len(scenes), 1.0 / math.sq...  8.28 us
    unnamed x23, local copies, waits for them, and re-layouts  5 us
    ppermute x2, starting transfers between devices, gather(): near = lax.ppermute(x, 'blk', xor1)  3.75 us
    ppermute x2, starting transfers between devices, gather(): far = lax.ppermute(x, 'blk', xor2)  3.02 us
    ppermute x2, waiting for transfers between devices, gather(): near = lax.ppermute(x, 'blk', xor1)  2.73 us
  transfers between devices with their start and end apart: 14, of which 4 were waited for; matrix products, arithmetic and copies ran while one was open for 3% of the time, Pallas kernels for 28%

profile of v1, /device:TPU:26, one launch (start us, length us, event | category | flops | bytes accessed | tf_op | source)
XLA Modules:
  0.0 96.6 jit_solution(5427104530651506583)
XLA Ops:
  0.6 0.4 collective-permute-start
  1.0 0.4 collective-permute-start.5
  1.5 0.7 collective-permute-start.2
  2.2 21.0 %collective-permute-done.refs_2_ = bf16[144,1536]{1,0:T(8,128)(2,1)S(1)} collective-permute-done((bf16[144,1536]{1,0:T(8,128)(2,1)}, bf16[144,1536]{1,0:T(8,128)(2,1)S(1)}, u32[]{:S(2)}, u32[]{:S(2)}) %collective-permute-start) | collective-permute-done | bytes 442400 | tf_op jit(solution)/shard_map/ppermute | solution.py:241
  23.2 1.3 %collective-permute-start.1 = (bf16[144,1536]{1,0:T(8,128)(2,1)S(1)}, bf16[144,1536]{1,0:T(8,128)(2,1)S(1)}, u32[]{:S(2)}, u32[]{:S(2)}) collective-permute-start(bf16[144,1536]{1,0:T(8,128)(2,1)S(1)} %collective-permute-done.refs_2_), channel_id=1, source_target_pairs={{8,0},{16,24},{9,1},{17,25},{10,2},{18,26},{11,3},{19,27},{12,4},{... | collective-permute-start | bytes 1327112 | tf_op jit(solution)/shard_map/ppermute | solution.py:243
  24.5 0.1 collective-permute-start.4
  24.6 0.9 constant_dynamic-update-slice_fusion.1
  25.5 0.9 constant_dynamic-update-slice_fusion.refs_0_
  26.4 2.6 %collective-permute-start.11 = (bf16[128,768]{1,0:T(8,128)(2,1)S(1)}, bf16[128,768]{1,0:T(8,128)(2,1)}, u32[]{:S(2)}, u32[]{:S(2)}) collective-permute-start(bf16[128,768]{1,0:T(8,128)(2,1)S(1)} %constant_dynamic-update-slice_fusion.refs_0_), channel_id=1, source_target_pairs={{0,16},{8,24},{16,0},{24,8},{1,17},{9,25},{17,1},{25,9},{2,18},{10... | collective-permute-start | bytes 589832 | tf_op jit(solution)/shard_map/ppermute | solution.py:241
  29.0 0.2 collective-permute-start.7
  29.2 12.1 %collective-permute-done.1 = bf16[144,1536]{1,0:T(8,128)(2,1)S(1)} collective-permute-done((bf16[144,1536]{1,0:T(8,128)(2,1)S(1)}, bf16[144,1536]{1,0:T(8,128)(2,1)S(1)}, u32[]{:S(2)}, u32[]{:S(2)}) %collective-permute-start.1) | collective-permute-done | bytes 442400 | tf_op jit(solution)/shard_map/ppermute | solution.py:243
  41.4 0.0 copy-start.3
  41.4 0.6 collective-permute-start.3
  42.0 1.0 %copy-done.1 = bf16[144,1536]{1,0:T(8,128)(2,1)S(1)} copy-done((bf16[144,1536]{1,0:T(8,128)(2,1)S(1)}, bf16[144,1536]{1,0:T(8,128)(2,1)}, u32[]{:S(2)}) %copy-start.1) | copy-done | bytes 442392
  43.0 0.7 copy-done.5
  43.7 0.7 copy-done.7
  44.4 0.7 copy-done.10
  45.0 8.2 %own.1 = (bf16[288,768]{1,0:T(8,128)(2,1)S(1)}, f32[288,128]{1,0:T(8,128)S(1)}, f32[288,768]{1,0:T(8,128)S(1)}) custom-call(bf16[144,1536]{1,0:T(8,128)(2,1)S(1)} %copy-done.1, bf16[144,1536]{1,0:T(8,128)(2,1)S(1)} %collective-permute-done.4.refs_1_.other_ref, f32[3,1536]{1,0:T(4,128)S(1)} %copy-done.5, bf16[3,1536,768]{2,1,0:T(8,128)(2,1)} %bitcast.10, ...), custom_call_target="tpu_custom_call" | custom-call | flops 2293235712 | bytes 7962624 | tf_op jit(solution)/shard_map/own/pallas_call | solution.py:168
  53.3 10.3 %more.1 = (f32[288,128]{1,0:T(8,128)S(1)}, f32[288,768]{1,0:T(8,128)S(1)}) custom-call(bf16[144,1536]{1,0:T(8,128)(2,1)S(1)} %collective-permute-done.5.refs_0_, bf16[144,1536]{1,0:T(8,128)(2,1)S(1)} %collective-permute-done.6.refs_1_, bf16[144,1536]{1,0:T(8,128)(2,1)S(1)} %collective-permute-done.refs_2_, ...), custom_call_target="tpu_custom_call" | custom-call | flops 3227516928 | bytes 8847360 | tf_op jit(solution)/shard_map/more/pallas_call | solution.py:168
  63.6 0.0 copy-start
  63.6 0.0 copy-start.2
  63.7 8.5 %last.1.ctx_ref = bf16[288,768]{1,0:T(8,128)(2,1)S(1)} custom-call(bf16[144,1536]{1,0:T(8,128)(2,1)S(1)} %broadcast_select_fusion.refs_0_, bf16[144,1536]{1,0:T(8,128)(2,1)S(1)} %collective-permute-done.3.refs_1_, f32[3,1536]{1,0:T(4,128)S(1)} %copy-done.6, bf16[3,1536,768]{2,1,0:T(8,128)(2,1)} %bitcast.12, f32[1,128]{1,0:T(1,128)S(1)} %bitcast.7, ...), custom_call_target="tpu_custom_call" | custom-call | flops 1613758464 | bytes 7962624 | tf_op jit(solution)/shard_map/last/pallas_call | solution.py:168
  72.2 0.1 collective-permute-start.8
  72.3 1.3 %collective-permute-start.13 = (bf16[128,768]{1,0:T(8,128)(2,1)S(1)}, bf16[128,768]{1,0:T(8,128)(2,1)}, u32[]{:S(2)}, u32[]{:S(2)}) collective-permute-start(bf16[128,768]{1,0:T(8,128)(2,1)S(1)} %constant_dynamic-update-slice_fusion.refs_0_), channel_id=1, source_target_pairs={{8,16},{16,8},{9,17},{17,9},{10,18},{18,10},{11,19},{19,11},{12,20... | collective-permute-start | bytes 589832 | tf_op jit(solution)/shard_map/ppermute | solution.py:242
  73.6 1.3 %collective-permute-start.12 = (bf16[128,768]{1,0:T(8,128)(2,1)}, bf16[128,768]{1,0:T(8,128)(2,1)}, u32[]{:S(2)}, u32[]{:S(2)}) collective-permute-start(bf16[128,768]{1,0:T(8,128)(2,1)} %collective-permute-done.11.refs_2_), channel_id=1, source_target_pairs={{8,0},{16,24},{9,1},{17,25},{10,2},{18,26},{11,3},{19,27},{12,4},{... | collective-permute-start | bytes 589832 | tf_op jit(solution)/shard_map/ppermute | solution.py:243
  74.9 3.3 %collective-permute-start.10 = (bf16[128,768]{1,0:T(8,128)(2,1)S(1)}, bf16[128,768]{1,0:T(8,128)(2,1)}, u32[]{:S(2)}, u32[]{:S(2)}) collective-permute-start(bf16[128,768]{1,0:T(8,128)(2,1)S(1)} %constant_dynamic-update-slice_fusion.refs_0_), channel_id=1, source_target_pairs={{0,8},{8,0},{16,24},{24,16},{1,9},{9,1},{17,25},{25,17},{2,10},{10... | collective-permute-start | bytes 589832 | tf_op jit(solution)/shard_map/ppermute | solution.py:240
  78.2 5.4 %collective-permute-done.12 = bf16[128,768]{1,0:T(8,128)(2,1)} collective-permute-done((bf16[128,768]{1,0:T(8,128)(2,1)}, bf16[128,768]{1,0:T(8,128)(2,1)}, u32[]{:S(2)}, u32[]{:S(2)}) %collective-permute-start.12) | collective-permute-done | bytes 196640 | tf_op jit(solution)/shard_map/ppermute | solution.py:243
  83.6 1.0 broadcast_select_fusion.1.refs_3_
  84.6 2.7 %collective-permute-done.10.refs_1_ = bf16[128,768]{1,0:T(8,128)(2,1)} collective-permute-done((bf16[128,768]{1,0:T(8,128)(2,1)S(1)}, bf16[128,768]{1,0:T(8,128)(2,1)}, u32[]{:S(2)}, u32[]{:S(2)}) %collective-permute-start.10) | collective-permute-done | bytes 196640 | tf_op jit(solution)/shard_map/ppermute | solution.py:240
  87.3 0.0 copy-start.4
  87.4 1.0 %copy-done.4 = bf16[144,1536]{1,0:T(8,128)(2,1)S(1)} copy-done((bf16[144,1536]{1,0:T(8,128)(2,1)S(1)}, bf16[144,1536]{1,0:T(8,128)(2,1)}, u32[]{:S(2)}) %copy-start.4) | copy-done | bytes 442392
  88.4 8.3 %final.1 = (bf16[144,1536]{1,0:T(8,128)(2,1)}, bf16[288,768]{1,0:T(8,128)(2,1)}) custom-call(s32[1]{0:T(128)} %bitcast.me_ref, bf16[288,768]{1,0:T(8,128)(2,1)S(1)} %last.1.ctx_ref, bf16[288,768]{1,0:T(8,128)(2,1)} %collective-permute-done.8.ctx_p_ref, bf16[144,1536]{1,0:T(8,128)(2,1)S(1)} %copy-done.2, bf16[144,1536]{1,0:T(8,128)(2,1)S(1)} %copy-done.4, ...), custom_call_target="tpu_custom_call" | custom-call | flops 2038431744 | bytes 7077888 | tf_op jit(solution)/shard_map/final/pallas_call | solution.py:195
  (26 shorter events, 0.1 us)
Async XLA Ops:
  0.6 22.6 %collective-permute-start = (bf16[144,1536]{1,0:T(8,128)(2,1)}, bf16[144,1536]{1,0:T(8,128)(2,1)S(1)}, u32[]{:S(2)}, u32[]{:S(2)}) collective-permute-start(bf16[144,1536]{1,0:T(8,128)(2,1)} %own_ref.1), channel_id=1, source_target_pairs={{0,16},{8,24},{16,0},{24,8},{1,17},{9,25},{17,1},{25,9},{2,18},{10... | collective-permute-start | bytes 1327112 | tf_op jit(solution)/shard_map/ppermute | solution.py:241
  1.0 86.3 %collective-permute-start.9 = (bf16[768,1536]{1,0:T(8,128)(2,1)}, bf16[768,1536]{1,0:T(8,128)(2,1)}, u32[]{:S(2)}, u32[]{:S(2)}) collective-permute-start(bf16[768,1536]{1,0:T(8,128)(2,1)} %wo_ref.1), channel_id=1, source_target_pairs={{0,4},{4,0},{1,5},{5,1},{2,6},{6,2},{3,7},{7,3},{8,12},{12,8},{9,1... | collective-permute-start | bytes 7077896 | tf_op jit(solution)/shard_map/ppermute | solution.py:218
  1.0 25.4 %collective-permute-start.5 = (bf16[144,1536]{1,0:T(8,128)(2,1)}, bf16[144,1536]{1,0:T(8,128)(2,1)S(1)}, u32[]{:S(2)}, u32[]{:S(2)}) collective-permute-start(bf16[144,1536]{1,0:T(8,128)(2,1)} %own_ref.1), channel_id=1, source_target_pairs={{0,8},{8,0},{16,24},{24,16},{1,9},{9,1},{17,25},{25,17},{2,10},{10... | collective-permute-start | bytes 1327112 | tf_op jit(solution)/shard_map/ppermute | solution.py:240
  1.5 27.5 %collective-permute-start.2 = (bf16[144,1536]{1,0:T(8,128)(2,1)}, bf16[144,1536]{1,0:T(8,128)(2,1)S(1)}, u32[]{:S(2)}, u32[]{:S(2)}) collective-permute-start(bf16[144,1536]{1,0:T(8,128)(2,1)} %own_ref.1), channel_id=1, source_target_pairs={{8,16},{16,8},{9,17},{17,9},{10,18},{18,10},{11,19},{19,11},{12,20... | collective-permute-start | bytes 1327112 | tf_op jit(solution)/shard_map/ppermute | solution.py:242
  23.2 18.1 %collective-permute-start.1 = (bf16[144,1536]{1,0:T(8,128)(2,1)S(1)}, bf16[144,1536]{1,0:T(8,128)(2,1)S(1)}, u32[]{:S(2)}, u32[]{:S(2)}) collective-permute-start(bf16[144,1536]{1,0:T(8,128)(2,1)S(1)} %collective-permute-done.refs_2_), channel_id=1, source_target_pairs={{8,0},{16,24},{9,1},{17,25},{10,2},{18,26},{11,3},{19,27},{12,4},{... | collective-permute-start | bytes 1327112 | tf_op jit(solution)/shard_map/ppermute | solution.py:243
  24.5 16.9 %collective-permute-start.4 = (bf16[144,1536]{1,0:T(8,128)(2,1)}, bf16[144,1536]{1,0:T(8,128)(2,1)S(1)}, u32[]{:S(2)}, u32[]{:S(2)}) collective-permute-start(bf16[144,1536]{1,0:T(8,128)(2,1)} %own_ref.1), channel_id=1, source_target_pairs={{0,4},{4,0},{1,5},{5,1},{2,6},{6,2},{3,7},{7,3},{8,12},{12,8},{9,1... | collective-permute-start | bytes 1327112 | tf_op jit(solution)/shard_map/ppermute | solution.py:218
  26.4 47.2 %collective-permute-start.11 = (bf16[128,768]{1,0:T(8,128)(2,1)S(1)}, bf16[128,768]{1,0:T(8,128)(2,1)}, u32[]{:S(2)}, u32[]{:S(2)}) collective-permute-start(bf16[128,768]{1,0:T(8,128)(2,1)S(1)} %constant_dynamic-update-slice_fusion.refs_0_), channel_id=1, source_target_pairs={{0,16},{8,24},{16,0},{24,8},{1,17},{9,25},{17,1},{25,9},{2,18},{10... | collective-permute-start | bytes 589832 | tf_op jit(solution)/shard_map/ppermute | solution.py:241
  29.0 24.2 %collective-permute-start.7 = (bf16[144,1536]{1,0:T(8,128)(2,1)S(1)}, bf16[144,1536]{1,0:T(8,128)(2,1)S(1)}, u32[]{:S(2)}, u32[]{:S(2)}) collective-permute-start(bf16[144,1536]{1,0:T(8,128)(2,1)S(1)} %collective-permute-done.refs_2_), channel_id=1, source_target_pairs={{0,4},{4,0},{1,5},{5,1},{2,6},{6,2},{3,7},{7,3},{8,12},{12,8},{9,1... | collective-permute-start | bytes 1327112 | tf_op jit(solution)/shard_map/ppermute | solution.py:218
  41.3 11.9 %collective-permute-start.6 = (bf16[144,1536]{1,0:T(8,128)(2,1)S(1)}, bf16[144,1536]{1,0:T(8,128)(2,1)S(1)}, u32[]{:S(2)}, u32[]{:S(2)}) collective-permute-start(bf16[144,1536]{1,0:T(8,128)(2,1)S(1)} %collective-permute-done.5.refs_0_), channel_id=1, source_target_pairs={{0,4},{4,0},{1,5},{5,1},{2,6},{6,2},{3,7},{7,3},{8,12},{12,8},{9,1... | collective-permute-start | bytes 1327112 | tf_op jit(solution)/shard_map/ppermute | solution.py:218
  41.4 11.8 %copy-start.3 = (bf16[144,1536]{1,0:T(8,128)(2,1)}, bf16[144,1536]{1,0:T(8,128)(2,1)S(1)}, u32[]{:S(2)}) copy-start(bf16[144,1536]{1,0:T(8,128)(2,1)S(1)} %collective-permute-done.4.refs_1_.other_ref) | copy-start | bytes 1327108
  41.4 22.2 %collective-permute-start.3 = (bf16[144,1536]{1,0:T(8,128)(2,1)S(1)}, bf16[144,1536]{1,0:T(8,128)(2,1)S(1)}, u32[]{:S(2)}, u32[]{:S(2)}) collective-permute-start(bf16[144,1536]{1,0:T(8,128)(2,1)S(1)} %broadcast_select_fusion.refs_0_), channel_id=1, source_target_pairs={{0,4},{4,0},{1,5},{5,1},{2,6},{6,2},{3,7},{7,3},{8,12},{12,8},{9,1... | collective-permute-start | bytes 1327112 | tf_op jit(solution)/shard_map/ppermute | solution.py:218
  42.0 1.0 %copy-start.1 = (bf16[144,1536]{1,0:T(8,128)(2,1)S(1)}, bf16[144,1536]{1,0:T(8,128)(2,1)}, u32[]{:S(2)}) copy-start(bf16[144,1536]{1,0:T(8,128)(2,1)} %own_ref.1) | copy-start | bytes 1327108
  43.0 0.7 copy-start.5
  43.7 0.7 copy-start.7
  44.4 0.7 copy-start.10
  45.0 8.2 %copy-start.6 = (f32[3,1536]{1,0:T(4,128)S(1)}, f32[3,1536]{1,0:T(4,128)}, u32[]{:S(2)}) copy-start(f32[3,1536]{1,0:T(4,128)} %mod_ref.1) | copy-start | bytes 55300
  45.0 8.2 %copy-start.8 = (f32[128]{0:T(128)S(1)}, f32[128]{0:T(128)}, u32[]{:S(2)}) copy-start(f32[128]{0:T(128)} %param.16) | copy-start | bytes 1540
  63.6 23.7 %copy-start = (bf16[768,1536]{1,0:T(8,128)(2,1)S(1)}, bf16[768,1536]{1,0:T(8,128)(2,1)}, u32[]{:S(2)}) copy-start(bf16[768,1536]{1,0:T(8,128)(2,1)} %wo_ref.1) | copy-start | bytes 7077892
  63.6 23.7 %copy-start.2 = (bf16[144,1536]{1,0:T(8,128)(2,1)S(1)}, bf16[144,1536]{1,0:T(8,128)(2,1)}, u32[]{:S(2)}) copy-start(bf16[144,1536]{1,0:T(8,128)(2,1)} %own_ref.1) | copy-start | bytes 1327108
  63.7 23.7 %copy-start.9 = (f32[128]{0:T(128)S(1)}, f32[128]{0:T(128)}, u32[]{:S(2)}) copy-start(f32[128]{0:T(128)} %param.17) | copy-start | bytes 1540
  72.2 15.1 %collective-permute-start.8 = (bf16[288,768]{1,0:T(8,128)(2,1)S(1)}, bf16[288,768]{1,0:T(8,128)(2,1)}, u32[]{:S(2)}, u32[]{:S(2)}) collective-permute-start(bf16[288,768]{1,0:T(8,128)(2,1)S(1)} %last.1.ctx_ref), channel_id=1, source_target_pairs={{0,4},{4,0},{1,5},{5,1},{2,6},{6,2},{3,7},{7,3},{8,12},{12,8},{9,1... | collective-permute-start | bytes 1327112 | tf_op jit(solution)/shard_map/ppermute | solution.py:218
  72.3 5.9 %collective-permute-start.13 = (bf16[128,768]{1,0:T(8,128)(2,1)S(1)}, bf16[128,768]{1,0:T(8,128)(2,1)}, u32[]{:S(2)}, u32[]{:S(2)}) collective-permute-start(bf16[128,768]{1,0:T(8,128)(2,1)S(1)} %constant_dynamic-update-slice_fusion.refs_0_), channel_id=1, source_target_pairs={{8,16},{16,8},{9,17},{17,9},{10,18},{18,10},{11,19},{19,11},{12,20... | collective-permute-start | bytes 589832 | tf_op jit(solution)/shard_map/ppermute | solution.py:242
  73.6 10.0 %collective-permute-start.12 = (bf16[128,768]{1,0:T(8,128)(2,1)}, bf16[128,768]{1,0:T(8,128)(2,1)}, u32[]{:S(2)}, u32[]{:S(2)}) collective-permute-start(bf16[128,768]{1,0:T(8,128)(2,1)} %collective-permute-done.11.refs_2_), channel_id=1, source_target_pairs={{8,0},{16,24},{9,1},{17,25},{10,2},{18,26},{11,3},{19,27},{12,4},{... | collective-permute-start | bytes 589832 | tf_op jit(solution)/shard_map/ppermute | solution.py:243
  74.9 12.4 %collective-permute-start.10 = (bf16[128,768]{1,0:T(8,128)(2,1)S(1)}, bf16[128,768]{1,0:T(8,128)(2,1)}, u32[]{:S(2)}, u32[]{:S(2)}) collective-permute-start(bf16[128,768]{1,0:T(8,128)(2,1)S(1)} %constant_dynamic-update-slice_fusion.refs_0_), channel_id=1, source_target_pairs={{0,8},{8,0},{16,24},{24,16},{1,9},{9,1},{17,25},{25,17},{2,10},{10... | collective-permute-start | bytes 589832 | tf_op jit(solution)/shard_map/ppermute | solution.py:240
  87.3 1.0 %copy-start.4 = (bf16[144,1536]{1,0:T(8,128)(2,1)S(1)}, bf16[144,1536]{1,0:T(8,128)(2,1)}, u32[]{:S(2)}) copy-start(bf16[144,1536]{1,0:T(8,128)(2,1)} %copy-done.3) | copy-start | bytes 1327108

commit v2 on v1

v2 whole, which is shorter than its diff:
```python
import functools
import math

import jax
import jax.numpy as jnp
from jax import lax
from jax.experimental import pallas as pl
from jax.experimental.pallas import tpu as pltpu
from jax.sharding import PartitionSpec as P


HD = 128
EPS = 1e-06


def modulate(rows, shift, scale):
    xfloat = rows.astype(jnp.float32)
    mean = jnp.mean(xfloat, axis=-1, keepdims=True)
    centred = xfloat - mean
    var = jnp.mean(centred * centred, axis=-1, keepdims=True)
    normed = centred * lax.rsqrt(var + EPS)
    return (normed * scale + shift).astype(jnp.bfloat16)


def piece_of(count, most):
    return max(p for p in range(16, most + 1, 16) if count % p == 0)


def head_norm(values, gain):
    rms = jnp.mean(values * values, axis=-1, keepdims=True)
    return (values * lax.rsqrt(rms + EPS) * gain).astype(jnp.bfloat16)


def dot(left, right):
    return jnp.dot(left, right, preferred_element_type=jnp.float32)


def dot_t(left, right):
    return lax.dot_general(
        left, right, (((1,), (1,)), ((), ())), preferred_element_type=jnp.float32
    )


def column_step(width):
    return 2 * HD if width % (2 * HD) == 0 else HD


def softmax_rows(scores_ref, weights_ref, rate, before=None):
    count = scores_ref.shape[0]
    step = piece_of(count, 32)
    bests, totals = [], []
    for r in range(0, count, step):
        scores = scores_ref[r : r + step, :]
        best = jnp.max(scores, axis=-1, keepdims=True)
        if before is not None:
            best = jnp.maximum(best, before[r : r + step])
        weights = jnp.exp2((scores - best) * rate)
        weights_ref[r : r + step, :] = weights.astype(jnp.bfloat16)
        bests.append(best)
        totals.append(jnp.sum(weights, axis=-1, keepdims=True))
    return jnp.concatenate(bests, axis=0), jnp.concatenate(totals, axis=0)


def blocks_kernel(n_rows, n_join, left_in, attend, first, carried, last, rate, *refs):
    refs = list(refs)

    def take(count):
        taken = refs[:count]
        del refs[:count]
        return taken

    row_refs = take(n_rows)
    join_refs = take(n_join)
    mod_ref, w_ref, kg_ref = take(3)
    if first:
        (qg_ref,) = take(1)
    else:
        q_ref, left_k, left_v = take(3)
        if carried:
            state_in, acc_in = take(2)
    if last:
        (ctx_ref,) = take(1)
    else:
        if first:
            (q_ref,) = take(1)
        out_k, out_v = take(2)
        if attend:
            state_out, acc_out = take(2)
    if n_join:
        (join_ref,) = take(1)
        at = 0
        for ref in join_refs:
            join_ref[at : at + ref.shape[0], :] = ref[...]
            at += ref.shape[0]
    rows_ref, k_ref, v_ref = take(3)
    if attend:
        scores_ref, weights_ref = take(2)
    shift = mod_ref[0:1, :]
    scale = 1.0 + mod_ref[1:2, :]
    at = 0
    for ref in row_refs:
        step = piece_of(ref.shape[0], 16)
        for r in range(0, ref.shape[0], step):
            rows_ref[at : at + step, :] = modulate(ref[r : r + step, :], shift, scale)
            at += step
    if left_in:
        k_ref[:left_in, :] = left_k[...]
        v_ref[:left_in, :] = left_v[...]
    width = w_ref.shape[2]
    wide = column_step(width)
    rows = rows_ref[...]
    for c in range(0, width, wide):
        span = slice(c, c + wide)
        k_wide = dot(rows, w_ref[1, :, span])
        v_ref[left_in:, span] = dot(rows, w_ref[2, :, span]).astype(jnp.bfloat16)
        if first:
            q_wide = dot(rows, w_ref[0, :, span])
        for j in range(0, wide, HD):
            h = (c + j) // HD
            lanes = slice(c + j, c + j + HD)
            k_ref[left_in:, lanes] = head_norm(k_wide[:, j : j + HD], kg_ref[...])
            if first:
                q_ref[:, lanes] = head_norm(q_wide[:, j : j + HD], qg_ref[...])
            if not attend:
                continue
            slot = h % 2
            scores_ref[slot] = dot_t(q_ref[:, lanes], k_ref[:attend, lanes])
            before = state_in[:, 2 * h : 2 * h + 1] if carried else None
            best, total = softmax_rows(
                scores_ref.at[slot], weights_ref.at[slot], rate, before
            )
            accum = dot(weights_ref[slot], v_ref[:attend, lanes])
            if carried:
                factor = jnp.exp2((before - best) * rate)
                total = total + factor * state_in[:, 2 * h + 1 : 2 * h + 2]
                accum = accum + factor * acc_in[:, lanes]
            if last:
                ctx_ref[:, lanes] = (accum / total).astype(jnp.bfloat16)
            else:
                state_out[:, 2 * h : 2 * h + 1] = best
                state_out[:, 2 * h + 1 : 2 * h + 2] = total
                acc_out[:, lanes] = accum
    if not last:
        out_k[...] = k_ref[attend:, :]
        out_v[...] = v_ref[attend:, :]


def final_kernel(
    n_scene, rate,
    me_ref, ctx_ref, ctx_p_ref, own_ref, other_ref, mod_ref, wo_ref, wo_p_ref, wc_ref, cg_ref, *refs
):
    scene_refs = refs[:n_scene]
    hidden_ref, out_ref, hid_ref, keys_ref, swap_ref, scores_ref, weights_ref, wp_ref, sem = refs[
        n_scene:
    ]
    copy = pltpu.make_async_copy(wo_p_ref, wp_ref, sem)
    copy.start()
    half = own_ref.shape[0]
    width = ctx_ref.shape[1]
    model = own_ref.shape[1]
    wide = column_step(width)
    swap_ref[:half, :] = ctx_p_ref[half:, :]
    swap_ref[half:, :] = ctx_p_ref[:half, :]
    each = scene_refs[0].shape[0] // 2
    for i, ref in enumerate(scene_refs):
        keys_ref[0, i * each : (i + 1) * each, :] = ref[:each, :]
        keys_ref[1, i * each : (i + 1) * each, :] = ref[each:, :]
    mine = ctx_ref[...]
    copy.wait()
    swapped = swap_ref[...]
    for c in range(0, model, wide):
        cols = slice(c, c + wide)
        attn = dot(mine, wo_ref[:, cols]) + dot(swapped, wp_ref[:, cols])
        gated = mod_ref[2:3, cols] * attn
        own = (own_ref[:, cols].astype(jnp.float32) + gated[:half]).astype(jnp.bfloat16)
        hidden_ref[:, cols] = own
        hid_ref[:half, cols] = own
        hid_ref[half:, cols] = (
            other_ref[:, cols].astype(jnp.float32) + gated[half:]
        ).astype(jnp.bfloat16)
    rows = hid_ref[...]
    me = me_ref[0]
    at_own = pl.multiple_of(me * half, half)
    at_other = pl.multiple_of((1 - me) * half, half)
    for c in range(0, width, wide):
        q_wide = dot(rows, wc_ref[:, c : c + wide])
        for j in range(0, wide, HD):
            slot = ((c + j) // HD) % 2
            lanes = slice(c + j, c + j + HD)
            queries = head_norm(q_wide[:, j : j + HD], cg_ref[...])
            scores_ref[slot] = dot_t(queries, keys_ref[0, :, lanes])
            _, total = softmax_rows(scores_ref.at[slot], weights_ref.at[slot], rate)
            accum = dot(weights_ref[slot], keys_ref[1, :, lanes])
            result = (accum / total).astype(jnp.bfloat16)
            out_ref[pl.ds(at_own, half), lanes] = result[:half]
            out_ref[pl.ds(at_other, half), lanes] = result[half:]


VM = pl.BlockSpec(memory_space=pltpu.VMEM)
SM = pl.BlockSpec(memory_space=pltpu.SMEM)
ANY = pl.BlockSpec(memory_space=pl.ANY)
PARAMS = pltpu.CompilerParams(vmem_limit_bytes=20 * 1024 * 1024)
RATE = math.log2(math.e) / math.sqrt(HD)


def blocks_call(row_list, join, mod, w3, q_gain, k_gain, carry, last):
    first = carry is None
    model = row_list[0].shape[1]
    fresh = sum(r.shape[0] for r in row_list)
    width = w3.shape[2]
    rows_q = fresh if first else carry[0].shape[0]
    left_in = 0 if first else carry[1].shape[0]
    carried = not first and len(carry) > 3
    keys = left_in + fresh
    if last:
        attend = keys
    else:
        attend = 0 if first else keys // HD * HD
    args = list(row_list) + list(join) + [mod, w3, k_gain]
    args += [q_gain] if first else list(carry)
    half = jnp.bfloat16
    shapes = []
    if last:
        shapes.append(((rows_q, width), half))
    else:
        if first:
            shapes.append(((rows_q, width), half))
        shapes += [((keys - attend, width), half)] * 2
        if attend:
            shapes += [((rows_q, HD), jnp.float32), ((rows_q, width), jnp.float32)]
    if join:
        shapes.append(((sum(r.shape[0] for r in join), width), half))
    scratch = [
        pltpu.VMEM((fresh, model), half),
        pltpu.VMEM((keys, width), half),
        pltpu.VMEM((keys, width), half),
    ]
    if attend:
        scratch += [
            pltpu.VMEM((2, rows_q, attend), jnp.float32),
            pltpu.VMEM((2, rows_q, attend), half),
        ]
    flops = 2 * fresh * model * width * (3 if first else 2) + 4 * rows_q * attend * width
    out = pl.pallas_call(
        functools.partial(
            blocks_kernel,
            len(row_list), len(join), left_in, attend, first, carried, last, RATE,
        ),
        out_shape=[jax.ShapeDtypeStruct(*s) for s in shapes],
        in_specs=[VM] * len(args),
        out_specs=[VM] * len(shapes),
        scratch_shapes=scratch,
        compiler_params=PARAMS,
        cost_estimate=pl.CostEstimate(
            flops=flops,
            transcendentals=rows_q * attend * width // HD,
            bytes_accessed=2 * fresh * model + 6 * model * width,
        ),
    )(*args)
    out = list(out)
    joined = out.pop() if join else None
    if last:
        return out[0], joined
    return (tuple(out) if first else (carry[0],) + tuple(out)), joined


def final_call(me, ctx, ctx_p, own, other, mod, wo, wo_p, wc, cg, scenes):
    half, model = own.shape
    rows, width = ctx.shape
    each = scenes[0].shape[0] // 2
    keys = each * len(scenes)
    args = [me, ctx, ctx_p, own, other, mod, wo, wo_p, wc, cg] + list(scenes)
    flops = 4 * rows * model * width + 2 * rows * model * width
    return pl.pallas_call(
        functools.partial(final_kernel, len(scenes), RATE),
        out_shape=[
            jax.ShapeDtypeStruct((half, model), jnp.bfloat16),
            jax.ShapeDtypeStruct((rows, width), jnp.bfloat16),
        ],
        in_specs=[SM] + [VM] * 6 + [ANY] + [VM] * (len(args) - 8),
        out_specs=[VM, VM],
        scratch_shapes=[
            pltpu.VMEM((rows, model), jnp.bfloat16),
            pltpu.VMEM((2, keys, width), jnp.bfloat16),
            pltpu.VMEM((rows, width), jnp.bfloat16),
            pltpu.VMEM((2, rows, keys), jnp.float32),
            pltpu.VMEM((2, rows, keys), jnp.bfloat16),
            pltpu.VMEM(wo_p.shape, jnp.bfloat16),
            pltpu.SemaphoreType.DMA(()),
        ],
        compiler_params=PARAMS,
        cost_estimate=pl.CostEstimate(
            flops=flops,
            transcendentals=rows * keys * width // HD,
            bytes_accessed=6 * model * width,
        ),
        name="final",
    )(*args)


def swap_cores(x):
    return lax.ppermute(x, "head", [(0, 1), (1, 0)])


def blk_permute(x, pairs):
    return lax.ppermute(x, "blk", pairs)


def body(
    tokens, modulation, w_qkv, w_out, w_cross, q_gain, k_gain, cross_gain, scene_keys, scene_values
):
    count = lax.axis_size("blk")
    me = lax.axis_index("head").astype(jnp.int32).reshape(1)
    place = lax.axis_index("blk")
    w3 = jnp.transpose(w_qkv, (1, 0, 2))
    q_gain, k_gain, cross_gain = (g.reshape(1, HD) for g in (q_gain, k_gain, cross_gain))
    other = swap_cores(tokens)
    w_out_p = swap_cores(w_out)
    at_end = (place == 0) | (place == count - 1)

    def gather(x):
        if count != 4:
            return [
                blk_permute(x, [(i, (i + s) % count) for i in range(count)])
                for s in range(1, count)
            ]
        near = blk_permute(x, [(i, i ^ 1) for i in range(4)])
        far = blk_permute(x, [(i, i ^ 2) for i in range(4)])
        mid = blk_permute(x, [(1, 2), (2, 1)])
        out = blk_permute(far, [(1, 0), (2, 3)])
        return [near, far, jnp.where(at_end, out, mid)]

    slots = gather(tokens)
    carry, scene = blocks_call(
        [tokens, other], [scene_keys, scene_values], modulation, w3, q_gain, k_gain,
        None, count == 1,
    )
    scenes = [scene] + gather(scene)
    pairs = [(x, swap_cores(x)) for x in slots]
    while pairs:
        taken, pairs = (pairs[:2], pairs[2:]) if len(pairs) > 1 else (pairs, [])
        carry, _ = blocks_call(
            [r for pair in taken for r in pair], [],
            modulation, w3, q_gain, k_gain, carry, not pairs,
        )
    ctx = carry
    ctx_p = swap_cores(ctx)
    hidden, cross_context = final_call(
        me, ctx, ctx_p, tokens, other, modulation, w_out, w_out_p, w_cross, cross_gain, scenes
    )
    return (hidden, cross_context)


def solution(mesh):
    return jax.shard_map(
        body,
        mesh=mesh,
        in_specs=(
            P(("clip", "blk", "head"), None),
            P("clip", None),
            P(None, None, "head"),
            P("head", None),
            P(None, "head"),
            P(),
            P(),
            P(),
            P(("clip", "blk"), "head"),
            P(("clip", "blk"), "head"),
        ),
        out_specs=(P(("clip", "blk", "head"), None), P(("clip", "blk"), "head")),
        check_vma=False,
    )
```

time: 97.1 us -> 91.6 us (0.943)
  the two profiles are of different devices: /device:TPU:26 before, /device:TPU:0 now
where the time goes in v2:
time: 91.6 us; the launch traced here: 91.1 us
  waiting for transfers between devices  37 us (40%)
  Pallas kernels  25.2 us (28%)
  starting transfers between devices  17.4 us (19%)
  local copies, waits for them, and re-layouts  9.56 us (10%)
  other arithmetic  1 us (1%)
  between operations  0.97 us (1%)
    ppermute x8, waiting for transfers between devices, blk_permute(): return lax.ppermute(x, 'blk', pairs)  37 us
    ppermute x8, starting transfers between devices, blk_permute(): return lax.ppermute(x, 'blk', pairs)  16.5 us
    pallas_call x3, Pallas kernels, blocks_call(): pl.pallas_call(functools.partial(blocks_kernel, len(row_list), len(join),...  16.4 us
    unnamed x28, local copies, waits for them, and re-layouts  9.56 us
    pallas_call x1, Pallas kernels, final_call(): pl.pallas_call(functools.partial(final_kernel, len(scenes), RATE), out_sh...  8.8 us
  transfers between devices with their start and end apart: 14, of which 4 were waited for; matrix products, arithmetic and copies ran while one was open for 1% of the time, Pallas kernels for 18%

profile of v2, /device:TPU:0, one launch (start us, length us, event | category | flops | bytes accessed | tf_op | source)
XLA Modules:
  0.0 91.1 jit_solution(7658997448862522873)
XLA Ops:
  0.6 4.1 %collective-permute-start = (bf16[144,1536]{1,0:T(8,128)(2,1)}, bf16[144,1536]{1,0:T(8,128)(2,1)S(1)}, u32[]{:S(2)}, u32[]{:S(2)}) collective-permute-start(bf16[144,1536]{1,0:T(8,128)(2,1)} %own_ref.1), channel_id=1, source_target_pairs={{0,16},{8,24},{16,0},{24,8},{1,17},{9,25},{17,1},{25,9},{2,18},{10... | collective-permute-start | bytes 1327112 | tf_op jit(solution)/shard_map/ppermute | solution.py:306
  4.8 1.6 %collective-permute-start.5 = (bf16[144,1536]{1,0:T(8,128)(2,1)}, bf16[144,1536]{1,0:T(8,128)(2,1)S(1)}, u32[]{:S(2)}, u32[]{:S(2)}) collective-permute-start(bf16[144,1536]{1,0:T(8,128)(2,1)} %own_ref.1), channel_id=1, source_target_pairs={{0,8},{8,0},{16,24},{24,16},{1,9},{9,1},{17,25},{25,17},{2,10},{10... | collective-permute-start | bytes 1327112 | tf_op jit(solution)/shard_map/ppermute | solution.py:306
  6.3 0.7 collective-permute-start.2
  7.0 18.5 %collective-permute-done.refs_2_ = bf16[144,1536]{1,0:T(8,128)(2,1)S(1)} collective-permute-done((bf16[144,1536]{1,0:T(8,128)(2,1)}, bf16[144,1536]{1,0:T(8,128)(2,1)S(1)}, u32[]{:S(2)}, u32[]{:S(2)}) %collective-permute-start) | collective-permute-done | bytes 442400 | tf_op jit(solution)/shard_map/ppermute | solution.py:306
  25.5 1.3 %collective-permute-start.1 = (bf16[144,1536]{1,0:T(8,128)(2,1)S(1)}, bf16[144,1536]{1,0:T(8,128)(2,1)S(1)}, u32[]{:S(2)}, u32[]{:S(2)}) collective-permute-start(bf16[144,1536]{1,0:T(8,128)(2,1)S(1)} %collective-permute-done.refs_2_), channel_id=1, source_target_pairs={{8,0},{16,24},{9,1},{17,25},{10,2},{18,26},{11,3},{19,27},{12,4},{... | collective-permute-start | bytes 1327112 | tf_op jit(solution)/shard_map/ppermute | solution.py:306
  26.8 0.1 collective-permute-start.4
  26.9 0.5 collective-permute-start.7
  27.4 0.1 collective-permute-start.6
  27.5 10.4 %collective-permute-done.1 = bf16[144,1536]{1,0:T(8,128)(2,1)S(1)} collective-permute-done((bf16[144,1536]{1,0:T(8,128)(2,1)S(1)}, bf16[144,1536]{1,0:T(8,128)(2,1)S(1)}, u32[]{:S(2)}, u32[]{:S(2)}) %collective-permute-start.1) | collective-permute-done | bytes 442400 | tf_op jit(solution)/shard_map/ppermute | solution.py:306
  37.9 0.1 collective-permute-start.3
  38.0 0.0 copy-start
  38.0 3.0 %copy-done = bf16[1536,3,768]{2,0,1:T(8,128)(2,1)S(1)} copy-done((bf16[1536,3,768]{2,0,1:T(8,128)(2,1)S(1)}, bf16[1536,3,768]{2,0,1:T(8,128)(2,1)}, u32[]{:S(2)}) %copy-start) | copy-done | bytes 7077912
  41.1 1.0 %copy-done.4 = bf16[144,1536]{1,0:T(8,128)(2,1)S(1)} copy-done((bf16[144,1536]{1,0:T(8,128)(2,1)S(1)}, bf16[144,1536]{1,0:T(8,128)(2,1)}, u32[]{:S(2)}) %copy-start.4) | copy-done | bytes 442392
  42.1 0.7 copy-done.6
  42.8 0.9 copy-done.8
  43.7 0.9 copy-done.9
  44.6 0.7 copy-done.10
  45.3 0.7 copy-done.12
  45.9 3.0 %shard_map.113 = (bf16[288,768]{1,0:T(8,128)(2,1)S(1)}, bf16[288,768]{1,0:T(8,128)(2,1)S(1)}, bf16[288,768]{1,0:T(8,128)(2,1)S(1)}, bf16[128,768]{1,0:T(8,128)(2,1)S(1)}) custom-call(bf16[144,1536]{1,0:T(8,128)(2,1)S(1)} %copy-done.4, bf16[144,1536]{1,0:T(8,128)(2,1)S(1)} %collective-permute-done.4.refs_1_.other_ref, bf16[64,768]{1,0:T(8,128)(2,1)S(1)} %copy-done.8, ...), custom_call_target="tpu_custom_call" | custom-call | flops 2038431744 | bytes 7962624 | tf_op jit(solution)/shard_map/pallas_call | solution.py:244
  48.9 2.4 %collective-permute-start.11 = (bf16[128,768]{1,0:T(8,128)(2,1)S(1)}, bf16[128,768]{1,0:T(8,128)(2,1)}, u32[]{:S(2)}, u32[]{:S(2)}) collective-permute-start(bf16[128,768]{1,0:T(8,128)(2,1)S(1)} %get-tuple-element.17.refs_0_), channel_id=1, source_target_pairs={{0,16},{8,24},{16,0},{24,8},{1,17},{9,25},{17,1},{25,9},{2,18},{10... | collective-permute-start | bytes 589832 | tf_op jit(solution)/shard_map/ppermute | solution.py:306
  51.4 6.9 %shard_map.114 = (bf16[96,768]{1,0:T(8,128)(2,1)S(1)}, bf16[96,768]{1,0:T(8,128)(2,1)S(1)}, f32[288,128]{1,0:T(8,128)S(1)}, f32[288,768]{1,0:T(8,128)S(1)}) custom-call(bf16[144,1536]{1,0:T(8,128)(2,1)S(1)} %collective-permute-done.5.refs_0_, bf16[144,1536]{1,0:T(8,128)(2,1)S(1)} %collective-permute-done.6.refs_1_, ...), custom_call_target="tpu_custom_call" | custom-call | flops 3397386240 | bytes 8847360 | tf_op jit(solution)/shard_map/pallas_call | solution.py:244
  58.2 0.0 copy-start.13
  58.2 6.5 %shard_map.115.ctx_ref = bf16[288,768]{1,0:T(8,128)(2,1)} custom-call(bf16[144,1536]{1,0:T(8,128)(2,1)S(1)} %broadcast_select_fusion.refs_0_, bf16[144,1536]{1,0:T(8,128)(2,1)S(1)} %collective-permute-done.3.refs_1_, f32[3,1536]{1,0:T(4,128)S(1)} %copy-done.6, bf16[3,1536,768]{2,1,0:T(8,128)(2,1)S(1)} %bitcast.7, f32[1,128]{1,0:T(1,128)S(1)} %bitcast.10, ...), custom_call_target="tpu_custom_call" | custom-call | flops 1698693120 | bytes 7962624 | tf_op jit(solution)/shard_map/pallas_call | solution.py:244
  64.8 0.2 collective-permute-start.8
  65.0 1.3 %collective-permute-start.13 = (bf16[128,768]{1,0:T(8,128)(2,1)S(1)}, bf16[128,768]{1,0:T(8,128)(2,1)}, u32[]{:S(2)}, u32[]{:S(2)}) collective-permute-start(bf16[128,768]{1,0:T(8,128)(2,1)S(1)} %get-tuple-element.17.refs_0_), channel_id=1, source_target_pairs={{8,16},{16,8},{9,17},{17,9},{10,18},{18,10},{11,19},{19,11},{12,20... | collective-permute-start | bytes 589832 | tf_op jit(solution)/shard_map/ppermute | solution.py:306
  66.3 1.3 %collective-permute-start.12 = (bf16[128,768]{1,0:T(8,128)(2,1)}, bf16[128,768]{1,0:T(8,128)(2,1)}, u32[]{:S(2)}, u32[]{:S(2)}) collective-permute-start(bf16[128,768]{1,0:T(8,128)(2,1)} %collective-permute-done.11.refs_2_), channel_id=1, source_target_pairs={{8,0},{16,24},{9,1},{17,25},{10,2},{18,26},{11,3},{19,27},{12,4},{... | collective-permute-start | bytes 589832 | tf_op jit(solution)/shard_map/ppermute | solution.py:306
  67.6 3.8 %collective-permute-start.10 = (bf16[128,768]{1,0:T(8,128)(2,1)S(1)}, bf16[128,768]{1,0:T(8,128)(2,1)S(1)}, u32[]{:S(2)}, u32[]{:S(2)}) collective-permute-start(bf16[128,768]{1,0:T(8,128)(2,1)S(1)} %get-tuple-element.17.refs_0_), channel_id=1, source_target_pairs={{0,8},{8,0},{16,24},{24,16},{1,9},{9,1},{17,25},{25,17},{2,10},{10... | collective-permute-start | bytes 589832 | tf_op jit(solution)/shard_map/ppermute | solution.py:306
  71.4 5.4 %collective-permute-done.12 = bf16[128,768]{1,0:T(8,128)(2,1)} collective-permute-done((bf16[128,768]{1,0:T(8,128)(2,1)}, bf16[128,768]{1,0:T(8,128)(2,1)}, u32[]{:S(2)}, u32[]{:S(2)}) %collective-permute-start.12) | collective-permute-done | bytes 196640 | tf_op jit(solution)/shard_map/ppermute | solution.py:306
  76.7 1.0 %broadcast_select_fusion.1.refs_3_ = bf16[128,768]{1,0:T(8,128)(2,1)S(1)} fusion(bf16[128,768]{1,0:T(8,128)(2,1)} %collective-permute-done.12, bf16[128,768]{1,0:T(8,128)(2,1)} %collective-permute-done.13, pred[]{:T(512)S(6)} %or.3), kind=kLoop, calls=%fused_computation.1 | loop fusion | flops 98304 | bytes 589825 | tf_op jit(solution)/shard_map/jit(_where)/select_n | solution.py:331
  77.7 2.8 %collective-permute-done.10.refs_1_ = bf16[128,768]{1,0:T(8,128)(2,1)S(1)} collective-permute-done((bf16[128,768]{1,0:T(8,128)(2,1)S(1)}, bf16[128,768]{1,0:T(8,128)(2,1)S(1)}, u32[]{:S(2)}, u32[]{:S(2)}) %collective-permute-start.10) | collective-permute-done | bytes 196640 | tf_op jit(solution)/shard_map/ppermute | solution.py:306
  80.5 1.7 %copy-done.3 = bf16[1536,768]{1,0:T(8,128)(2,1)S(1)} copy-done((bf16[1536,768]{1,0:T(8,128)(2,1)S(1)}, bf16[1536,768]{1,0:T(8,128)(2,1)}, u32[]{:S(2)}) %copy-start.3) | copy-done | bytes 2359320
  82.2 8.8 %final.1 = (bf16[144,1536]{1,0:T(8,128)(2,1)}, bf16[288,768]{1,0:T(8,128)(2,1)}) custom-call(s32[1]{0:T(128)} %bitcast.me_ref, bf16[288,768]{1,0:T(8,128)(2,1)} %shard_map.115.ctx_ref, bf16[288,768]{1,0:T(8,128)(2,1)} %collective-permute-done.8.ctx_p_ref, bf16[144,1536]{1,0:T(8,128)(2,1)S(1)} %copy-done.5, ...), custom_call_target="tpu_custom_call" | custom-call | flops 2038431744 | bytes 7077888 | tf_op jit(solution)/shard_map/final/pallas_call | solution.py:274
  (30 shorter events, 0.1 us)
Async XLA Ops:
  0.6 24.9 %collective-permute-start = (bf16[144,1536]{1,0:T(8,128)(2,1)}, bf16[144,1536]{1,0:T(8,128)(2,1)S(1)}, u32[]{:S(2)}, u32[]{:S(2)}) collective-permute-start(bf16[144,1536]{1,0:T(8,128)(2,1)} %own_ref.1), channel_id=1, source_target_pairs={{0,16},{8,24},{16,0},{24,8},{1,17},{9,25},{17,1},{25,9},{2,18},{10... | collective-permute-start | bytes 1327112 | tf_op jit(solution)/shard_map/ppermute | solution.py:306
  4.8 75.7 %collective-permute-start.9 = (bf16[768,1536]{1,0:T(8,128)(2,1)}, bf16[768,1536]{1,0:T(8,128)(2,1)}, u32[]{:S(2)}, u32[]{:S(2)}) collective-permute-start(bf16[768,1536]{1,0:T(8,128)(2,1)} %wo_ref.1), channel_id=1, source_target_pairs={{0,4},{4,0},{1,5},{5,1},{2,6},{6,2},{3,7},{7,3},{8,12},{12,8},{9,1... | collective-permute-start | bytes 7077896 | tf_op jit(solution)/shard_map/ppermute | solution.py:302
  4.8 22.1 %collective-permute-start.5 = (bf16[144,1536]{1,0:T(8,128)(2,1)}, bf16[144,1536]{1,0:T(8,128)(2,1)S(1)}, u32[]{:S(2)}, u32[]{:S(2)}) collective-permute-start(bf16[144,1536]{1,0:T(8,128)(2,1)} %own_ref.1), channel_id=1, source_target_pairs={{0,8},{8,0},{16,24},{24,16},{1,9},{9,1},{17,25},{25,17},{2,10},{10... | collective-permute-start | bytes 1327112 | tf_op jit(solution)/shard_map/ppermute | solution.py:306
  6.3 21.0 %collective-permute-start.2 = (bf16[144,1536]{1,0:T(8,128)(2,1)}, bf16[144,1536]{1,0:T(8,128)(2,1)S(1)}, u32[]{:S(2)}, u32[]{:S(2)}) collective-permute-start(bf16[144,1536]{1,0:T(8,128)(2,1)} %own_ref.1), channel_id=1, source_target_pairs={{8,16},{16,8},{9,17},{17,9},{10,18},{18,10},{11,19},{19,11},{12,20... | collective-permute-start | bytes 1327112 | tf_op jit(solution)/shard_map/ppermute | solution.py:306
  25.5 12.4 %collective-permute-start.1 = (bf16[144,1536]{1,0:T(8,128)(2,1)S(1)}, bf16[144,1536]{1,0:T(8,128)(2,1)S(1)}, u32[]{:S(2)}, u32[]{:S(2)}) collective-permute-start(bf16[144,1536]{1,0:T(8,128)(2,1)S(1)} %collective-permute-done.refs_2_), channel_id=1, source_target_pairs={{8,0},{16,24},{9,1},{17,25},{10,2},{18,26},{11,3},{19,27},{12,4},{... | collective-permute-start | bytes 1327112 | tf_op jit(solution)/shard_map/ppermute | solution.py:306
  26.8 11.2 %collective-permute-start.4 = (bf16[144,1536]{1,0:T(8,128)(2,1)}, bf16[144,1536]{1,0:T(8,128)(2,1)S(1)}, u32[]{:S(2)}, u32[]{:S(2)}) collective-permute-start(bf16[144,1536]{1,0:T(8,128)(2,1)} %own_ref.1), channel_id=1, source_target_pairs={{0,4},{4,0},{1,5},{5,1},{2,6},{6,2},{3,7},{7,3},{8,12},{12,8},{9,1... | collective-permute-start | bytes 1327112 | tf_op jit(solution)/shard_map/ppermute | solution.py:302
  26.9 24.4 %collective-permute-start.7 = (bf16[144,1536]{1,0:T(8,128)(2,1)S(1)}, bf16[144,1536]{1,0:T(8,128)(2,1)S(1)}, u32[]{:S(2)}, u32[]{:S(2)}) collective-permute-start(bf16[144,1536]{1,0:T(8,128)(2,1)S(1)} %collective-permute-done.refs_2_), channel_id=1, source_target_pairs={{0,4},{4,0},{1,5},{5,1},{2,6},{6,2},{3,7},{7,3},{8,12},{12,8},{9,1... | collective-permute-start | bytes 1327112 | tf_op jit(solution)/shard_map/ppermute | solution.py:302
  27.4 23.9 %collective-permute-start.6 = (bf16[144,1536]{1,0:T(8,128)(2,1)S(1)}, bf16[144,1536]{1,0:T(8,128)(2,1)S(1)}, u32[]{:S(2)}, u32[]{:S(2)}) collective-permute-start(bf16[144,1536]{1,0:T(8,128)(2,1)S(1)} %collective-permute-done.5.refs_0_), channel_id=1, source_target_pairs={{0,4},{4,0},{1,5},{5,1},{2,6},{6,2},{3,7},{7,3},{8,12},{12,8},{9,1... | collective-permute-start | bytes 1327112 | tf_op jit(solution)/shard_map/ppermute | solution.py:302
  37.9 20.3 %collective-permute-start.3 = (bf16[144,1536]{1,0:T(8,128)(2,1)S(1)}, bf16[144,1536]{1,0:T(8,128)(2,1)S(1)}, u32[]{:S(2)}, u32[]{:S(2)}) collective-permute-start(bf16[144,1536]{1,0:T(8,128)(2,1)S(1)} %broadcast_select_fusion.refs_0_), channel_id=1, source_target_pairs={{0,4},{4,0},{1,5},{5,1},{2,6},{6,2},{3,7},{7,3},{8,12},{12,8},{9,1... | collective-permute-start | bytes 1327112 | tf_op jit(solution)/shard_map/ppermute | solution.py:302
  38.0 3.0 %copy-start = (bf16[1536,3,768]{2,0,1:T(8,128)(2,1)S(1)}, bf16[1536,3,768]{2,0,1:T(8,128)(2,1)}, u32[]{:S(2)}) copy-start(bf16[1536,3,768]{2,0,1:T(8,128)(2,1)} %param.12) | copy-start | bytes 21233668
  41.1 1.0 %copy-start.4 = (bf16[144,1536]{1,0:T(8,128)(2,1)S(1)}, bf16[144,1536]{1,0:T(8,128)(2,1)}, u32[]{:S(2)}) copy-start(bf16[144,1536]{1,0:T(8,128)(2,1)} %own_ref.1) | copy-start | bytes 1327108
  42.1 0.7 copy-start.6
  42.8 0.9 copy-start.8
  43.7 0.9 copy-start.9
  44.6 0.7 copy-start.10
  45.2 0.7 copy-start.12
  45.9 5.4 %copy-start.1 = (bf16[1536,3,768]{2,0,1:T(8,128)(2,1)S(1)}, bf16[1536,3,768]{2,0,1:T(8,128)(2,1)}, u32[]{:S(2)}) copy-start(bf16[1536,3,768]{2,0,1:T(8,128)(2,1)} %param.12) | copy-start | bytes 21233668
  45.9 5.4 %copy-start.11 = (f32[128]{0:T(128)S(1)}, f32[128]{0:T(128)}, u32[]{:S(2)}) copy-start(f32[128]{0:T(128)} %param.16) | copy-start | bytes 1540
  48.9 17.4 %collective-permute-start.11 = (bf16[128,768]{1,0:T(8,128)(2,1)S(1)}, bf16[128,768]{1,0:T(8,128)(2,1)}, u32[]{:S(2)}, u32[]{:S(2)}) collective-permute-start(bf16[128,768]{1,0:T(8,128)(2,1)S(1)} %get-tuple-element.17.refs_0_), channel_id=1, source_target_pairs={{0,16},{8,24},{16,0},{24,8},{1,17},{9,25},{17,1},{25,9},{2,18},{10... | collective-permute-start | bytes 589832 | tf_op jit(solution)/shard_map/ppermute | solution.py:306
  58.2 22.3 %copy-start.2 = (bf16[768,1536]{1,0:T(8,128)(2,1)S(1)}, bf16[768,1536]{1,0:T(8,128)(2,1)}, u32[]{:S(2)}) copy-start(bf16[768,1536]{1,0:T(8,128)(2,1)} %wo_ref.1) | copy-start | bytes 7077892
  58.2 22.3 %copy-start.5 = (bf16[144,1536]{1,0:T(8,128)(2,1)S(1)}, bf16[144,1536]{1,0:T(8,128)(2,1)}, u32[]{:S(2)}) copy-start(bf16[144,1536]{1,0:T(8,128)(2,1)} %own_ref.1) | copy-start | bytes 1327108
  58.2 22.3 %copy-start.7 = (f32[3,1536]{1,0:T(4,128)S(1)}, f32[3,1536]{1,0:T(4,128)}, u32[]{:S(2)}) copy-start(f32[3,1536]{1,0:T(4,128)} %mod_ref.1) | copy-start | bytes 55300
  58.2 22.3 %copy-start.13 = (f32[128]{0:T(128)S(1)}, f32[128]{0:T(128)}, u32[]{:S(2)}) copy-start(f32[128]{0:T(128)} %param.17) | copy-start | bytes 1540
  64.8 15.7 %collective-permute-start.8 = (bf16[288,768]{1,0:T(8,128)(2,1)}, bf16[288,768]{1,0:T(8,128)(2,1)}, u32[]{:S(2)}, u32[]{:S(2)}) collective-permute-start(bf16[288,768]{1,0:T(8,128)(2,1)} %shard_map.115.ctx_ref), channel_id=1, source_target_pairs={{0,4},{4,0},{1,5},{5,1},{2,6},{6,2},{3,7},{7,3},{8,12},{12,8},{9,1... | collective-permute-start | bytes 1327112 | tf_op jit(solution)/shard_map/ppermute | solution.py:302
  65.0 6.4 %collective-permute-start.13 = (bf16[128,768]{1,0:T(8,128)(2,1)S(1)}, bf16[128,768]{1,0:T(8,128)(2,1)}, u32[]{:S(2)}, u32[]{:S(2)}) collective-permute-start(bf16[128,768]{1,0:T(8,128)(2,1)S(1)} %get-tuple-element.17.refs_0_), channel_id=1, source_target_pairs={{8,16},{16,8},{9,17},{17,9},{10,18},{18,10},{11,19},{19,11},{12,20... | collective-permute-start | bytes 589832 | tf_op jit(solution)/shard_map/ppermute | solution.py:306
  66.3 10.4 %collective-permute-start.12 = (bf16[128,768]{1,0:T(8,128)(2,1)}, bf16[128,768]{1,0:T(8,128)(2,1)}, u32[]{:S(2)}, u32[]{:S(2)}) collective-permute-start(bf16[128,768]{1,0:T(8,128)(2,1)} %collective-permute-done.11.refs_2_), channel_id=1, source_target_pairs={{8,0},{16,24},{9,1},{17,25},{10,2},{18,26},{11,3},{19,27},{12,4},{... | collective-permute-start | bytes 589832 | tf_op jit(solution)/shard_map/ppermute | solution.py:306
  67.6 12.8 %collective-permute-start.10 = (bf16[128,768]{1,0:T(8,128)(2,1)S(1)}, bf16[128,768]{1,0:T(8,128)(2,1)S(1)}, u32[]{:S(2)}, u32[]{:S(2)}) collective-permute-start(bf16[128,768]{1,0:T(8,128)(2,1)S(1)} %get-tuple-element.17.refs_0_), channel_id=1, source_target_pairs={{0,8},{8,0},{16,24},{24,16},{1,9},{9,1},{17,25},{25,17},{2,10},{10... | collective-permute-start | bytes 589832 | tf_op jit(solution)/shard_map/ppermute | solution.py:306
  80.5 1.7 %copy-start.3 = (bf16[1536,768]{1,0:T(8,128)(2,1)S(1)}, bf16[1536,768]{1,0:T(8,128)(2,1)}, u32[]{:S(2)}) copy-start(bf16[1536,768]{1,0:T(8,128)(2,1)} %wc_ref.1) | copy-start | bytes 7077892
